TPU v7x, 256 devices: a whole 4x4x8 slice. The times are simulated.
256 devices in a mesh: slab: 64 (over y, x_hi, z), sub: 4 (over x_lo, core).
Axes of the slice: x: 4 (x_hi: 2, x_lo: 2; x = x_hi * 2 + x_lo), y: 4, z: 8, core: 2. Of those that a mesh axis runs over, the one named last changes fastest.
Arguments:
- right_sides: bfloat16 [524288, 768], P(('slab', 'sub')), may hold values from -6 to 6
- front_sides: bfloat16 [131072, 768], P(('slab', 'sub')), may hold values from -6 to 6
- pending_front: bfloat16 [131072, 256], P(('slab', 'sub')), may hold values from -6 to 6
- inner_index: int32 [4096, 6], P(('slab', 'sub')), may hold values from 0 to 15, all different within a row
- inner_blocks: bfloat16 [4096, 6, 128, 128], P(('slab', 'sub')), may hold values from -0.15625 to 0.15625
- inner_inverse: bfloat16 [4096, 128, 128], P(('slab', 'sub')), may hold values from -1 to 2
- outer_index: int32 [1024, 8], P(('slab', 'sub')), may hold values from 0 to 15, all different within a row
- outer_blocks: bfloat16 [1024, 8, 128, 128], P(('slab', 'sub')), may hold values from -0.125 to 0.125
- front_inverse: bfloat16 [1024, 128, 128], P(('slab', 'sub')), may hold values from -1 to 2
Outputs:
- solution: bfloat16 [524288, 768], P(('slab', 'sub'))
- front_solution: bfloat16 [131072, 768], P(('slab', 'sub'))
All inputs are finite; a program needn't handle non-finite values.
Results may differ from a plain program's by a relative error of at most 0.009.
Values may be sent and summed in bfloat16 or wider, within the bound.
A program may use at most 64 MiB of HBM per device.

v0:
```python
import jax
import jax.numpy as jnp
from jax import lax
from jax.sharding import PartitionSpec as P


def passed_along(x, axis, by):
    size = lax.axis_size(axis)
    pairs = [(i, i + by) for i in range(size) if 0 <= i + by < size]
    return lax.ppermute(x, axis, pairs)


def collect(share):
    return lax.all_gather(share, "sub", axis=0, tiled=True)


def shards(
    right_sides,
    front_sides,
    pending_front,
    inner_index,
    inner_blocks,
    inner_inverse,
    outer_index,
    outer_blocks,
    front_inverse,
):
    block_size = inner_inverse.shape[1]
    inner_rows = inner_inverse.shape[0]
    outer_rows = front_inverse.shape[0]
    columns = pending_front.shape[1]
    groups = right_sides.shape[1] // columns
    gathered = collect(pending_front)
    solved_list = []
    front_list = []
    for group in range(groups):
        front_blocks = gathered.reshape(-1, block_size, columns)
        picked = jnp.take(front_blocks, inner_index, axis=0)
        coupled = jnp.einsum(
            "ikab,ikbc->iac", inner_blocks, picked, preferred_element_type=jnp.float32
        )
        group_sides = right_sides[:, group * columns : (group + 1) * columns].reshape(
            inner_rows, block_size, columns
        )
        inner_values = (group_sides.astype(jnp.float32) - coupled).astype(jnp.bfloat16)
        solved = jnp.einsum(
            "iab,ibc->iac", inner_inverse, inner_values, preferred_element_type=jnp.float32
        ).astype(jnp.bfloat16)
        chosen = jnp.take(solved, outer_index, axis=0)
        outgoing = jnp.einsum(
            "jkab,jkbc->jac", outer_blocks, chosen, preferred_element_type=jnp.float32
        )
        outer_sides = front_sides[:, group * columns : (group + 1) * columns].reshape(
            outer_rows, block_size, columns
        )
        outer_values = (outer_sides.astype(jnp.float32) - outgoing).astype(jnp.bfloat16)
        front_done = jnp.einsum(
            "jab,jbc->jac", front_inverse, outer_values, preferred_element_type=jnp.float32
        ).astype(jnp.bfloat16)
        front_done = front_done.reshape(-1, columns)
        solved_list.append(solved.reshape(-1, columns))
        front_list.append(front_done)
        if group + 1 < groups:
            gathered = passed_along(collect(front_done), "slab", 1)
    solution = jnp.concatenate(solved_list, axis=1)
    front_solution = jnp.concatenate(front_list, axis=1)
    return (solution, front_solution)


def solution(mesh):
    placed = (
        P(("slab", "sub"), None),
        P(("slab", "sub"), None),
        P(("slab", "sub"), None),
        P(("slab", "sub"), None),
        P(("slab", "sub"), None, None, None),
        P(("slab", "sub"), None, None),
        P(("slab", "sub"), None),
        P(("slab", "sub"), None, None, None),
        P(("slab", "sub"), None, None),
    )
    return jax.shard_map(
        shards,
        mesh=mesh,
        in_specs=placed,
        out_specs=(P(("slab", "sub"), None), P(("slab", "sub"), None)),
        check_vma=False,
    )
```

profile of v0, /device:TPU:9, one launch (start us, length us, event | category | flops | bytes accessed | tf_op | source)
XLA Modules:
  0.0 216.6 jit_solution(2010275956903110285)
XLA Ops:
  7.2 0.0 copy-start
  7.2 0.0 all-gather.4.cloned.1.call-start
  7.2 0.7 all-gather.4.cloned.1.call-update
  7.9 0.0 all-gather.6.cloned.1.call-start
  8.0 0.8 compare_and_fusion
  8.8 0.7 compare_select_fusion.1
  9.5 0.1 copy.17
  9.6 0.1 reshape.138
  9.7 0.7 compare_select_fusion
  10.4 0.1 copy.18
  10.5 0.1 reshape.134
  10.6 0.7 compare_and_fusion.1
  11.3 2.0 fusion.115
  13.2 3.6 %fusion.114 = (bf16[2048,256]{1,0:T(8,128)(2,1)}, bf16[2048,256]{1,0:T(8,128)(2,1)}, bf16[2048,256]{1,0:T(8,128)(2,1)}) fusion(bf16[2048,768]{1,0:T(8,128)(2,1)} %param.13), kind=kLoop, calls=%fused_computation.74 | loop fusion | bytes 6291456 | tf_op jit(solution)/shard_map/slice | solution.py:42
  16.8 19.5 %all-gather.4.cloned.1.call-done = bf16[2048,256]{1,0:T(8,128)(2,1)} async-done(((bf16[512,256]{1,0:T(8,128)(2,1)}), bf16[2048,256]{1,0:T(8,128)(2,1)}) %all-gather.4.cloned.1.call-update) | async-done | bytes 1048592 | tf_op jit(solution)/shard_map/all_gather | solution.py:14
  36.3 7.2 %gather_fusion = bf16[96,128,256]{2,1,0:T(8,128)(2,1)} fusion(bf16[16,128,256]{2,1,0:T(8,128)(2,1)} %bitcast.123, s32[1024]{0:T(1024)S(1)} %pad_clamp_fusion.1), kind=kCustom, calls=%fused_computation.clone | custom fusion | bytes 12583296 | tf_op jit(solution)/shard_map/jit(_take)/gather | solution.py:38
  43.5 0.0 copy-done
  43.5 6.0 %fusion.45 = bf16[16,256,128]{1,2,0:T(8,128)(2,1)} fusion(bf16[16,128,128]{2,1,0:T(8,128)(2,1)} %param.18, bf16[16,128,256]{2,1,0:T(8,128)(2,1)} %bitcast.142, bf16[16,6,128,128]{3,2,1,0:T(8,128)(2,1)S(1)} %copy-done, bf16[16,6,128,256]{3,2,1,0:T(8,128)(2,1)} %bitcast.131, pred[16,6]{1,0:T(8,128)(4,1)S(1)} %copy.17), kind=kOutput, calls=%fused_computation.39 | convolution fusion | flops 944766976 | bytes 12058720 | tf_op jit(solution)/shard_map/iab,ibc->iac/dot_general | solution.py:46
  49.6 0.0 copy-start.2
  49.6 3.3 %gather_fusion.1 = bf16[32,128,256]{2,1,0:T(8,128)(2,1)} fusion(bf16[16,128,256]{2,1,0:T(8,128)(2,1)} %bitcast.124, s32[1024]{0:T(1024)S(1)} %pad_clamp_fusion), kind=kCustom, calls=%fused_computation.1.clone | custom fusion | bytes 4194432 | tf_op jit(solution)/shard_map/jit(_take)/gather | solution.py:49
  52.8 0.0 copy-done.2
  52.8 3.4 %fusion.90 = bf16[4,256,128]{1,2,0:T(8,128)(2,1)} fusion(bf16[4,128,128]{2,1,0:T(8,128)(2,1)S(1)} %copy-done.2, bf16[4,8,128,128]{3,2,1,0:T(8,128)(2,1)} %param.20, bf16[4,8,128,256]{3,2,1,0:T(8,128)(2,1)} %bitcast.134, pred[4,8]{1,0:T(4,128)(4,1)S(1)} %compare_and_fusion.1, bf16[4,128,256]{2,1,0:T(8,128)(2,1)} %bitcast.145), kind=kOutput, calls=%fused_computation.54 | convolution fusion | flops 303562752 | bytes 3801120 | tf_op jit(solution)/shard_map/jab,jbc->jac/dot_general | solution.py:57
  56.2 0.0 all-gather.6.cloned.1.call-update
  56.3 0.0 all-gather.8.cloned.1.call-start
  56.3 24.2 %all-gather.6.cloned.1.call-done = bf16[2048,256]{1,0:T(8,128)(2,1)} async-done(((bf16[512,256]{1,0:T(8,128)(2,1)}), bf16[2048,256]{1,0:T(8,128)(2,1)}) %all-gather.6.cloned.1.call-update) | async-done | bytes 1048592 | tf_op jit(solution)/shard_map/all_gather | solution.py:14
  80.5 3.2 %collective-permute-start = (bf16[2048,256]{1,0:T(8,128)(2,1)}, bf16[2048,256]{1,0:T(8,128)(2,1)}, u32[]{:S(2)}, u32[]{:S(2)}) collective-permute-start(bf16[2048,256]{1,0:T(8,128)(2,1)} %all-gather.6.cloned.1.call-done), channel_id=1, source_target_pairs={{0,4},{4,8},{8,12},{12,16},{16,20},{20,24},{24,28},{28,32},{32,36}... | collective-permute-start | bytes 3145736 | tf_op jit(solution)/shard_map/ppermute | solution.py:10
  83.7 28.4 %collective-permute-done = bf16[2048,256]{1,0:T(8,128)(2,1)} collective-permute-done((bf16[2048,256]{1,0:T(8,128)(2,1)}, bf16[2048,256]{1,0:T(8,128)(2,1)}, u32[]{:S(2)}, u32[]{:S(2)}) %collective-permute-start) | collective-permute-done | bytes 1048608 | tf_op jit(solution)/shard_map/ppermute | solution.py:10
  112.1 7.2 %gather_fusion.2 = bf16[96,128,256]{2,1,0:T(8,128)(2,1)} fusion(bf16[16,128,256]{2,1,0:T(8,128)(2,1)} %bitcast.16, s32[1024]{0:T(1024)S(1)} %pad_clamp_fusion.1), kind=kCustom, calls=%fused_computation.2.clone | custom fusion | bytes 12583296 | tf_op jit(solution)/shard_map/jit(_take)/gather | solution.py:38
  119.3 6.1 %fusion.42 = bf16[16,256,128]{1,2,0:T(8,128)(2,1)} fusion(bf16[16,128,128]{2,1,0:T(8,128)(2,1)} %param.18, bf16[16,128,256]{2,1,0:T(8,128)(2,1)} %bitcast.141, bf16[16,6,128,128]{3,2,1,0:T(8,128)(2,1)S(1)} %copy-done, bf16[16,6,128,256]{3,2,1,0:T(8,128)(2,1)} %bitcast.132, pred[16,6]{1,0:T(8,128)(4,1)S(1)} %copy.17), kind=kOutput, calls=%fused_computation.38 | convolution fusion | flops 944766976 | bytes 12058720 | tf_op jit(solution)/shard_map/iab,ibc->iac/dot_general | solution.py:46
  125.4 3.2 %gather_fusion.3 = bf16[32,128,256]{2,1,0:T(8,128)(2,1)} fusion(bf16[16,128,256]{2,1,0:T(8,128)(2,1)} %bitcast.126, s32[1024]{0:T(1024)S(1)} %pad_clamp_fusion), kind=kCustom, calls=%fused_computation.4.clone | custom fusion | bytes 4194432 | tf_op jit(solution)/shard_map/jit(_take)/gather | solution.py:49
  128.6 3.4 %fusion.87 = bf16[4,256,128]{1,2,0:T(8,128)(2,1)} fusion(bf16[4,128,128]{2,1,0:T(8,128)(2,1)S(1)} %copy-done.2, bf16[4,8,128,128]{3,2,1,0:T(8,128)(2,1)} %param.20, bf16[4,8,128,256]{3,2,1,0:T(8,128)(2,1)} %bitcast.135, pred[4,8]{1,0:T(4,128)(4,1)S(1)} %compare_and_fusion.1, bf16[4,128,256]{2,1,0:T(8,128)(2,1)S(1)} %bitcast.144), kind=kOutput, calls=%fused_computation.53 | convolution fusion | flops 303562752 | bytes 3801120 | tf_op jit(solution)/shard_map/jab,jbc->jac/dot_general | solution.py:57
  132.0 0.0 all-gather.8.cloned.1.call-update
  132.1 21.4 %all-gather.8.cloned.1.call-done = bf16[2048,256]{1,0:T(8,128)(2,1)} async-done(((bf16[512,256]{1,0:T(8,128)(2,1)}), bf16[2048,256]{1,0:T(8,128)(2,1)}) %all-gather.8.cloned.1.call-update) | async-done | bytes 1048592 | tf_op jit(solution)/shard_map/all_gather | solution.py:14
  153.5 3.4 %collective-permute-start.1 = (bf16[2048,256]{1,0:T(8,128)(2,1)}, bf16[2048,256]{1,0:T(8,128)(2,1)}, u32[]{:S(2)}, u32[]{:S(2)}) collective-permute-start(bf16[2048,256]{1,0:T(8,128)(2,1)} %all-gather.8.cloned.1.call-done), channel_id=1, source_target_pairs={{0,4},{4,8},{8,12},{12,16},{16,20},{20,24},{24,28},{28,32},{32,36}... | collective-permute-start | bytes 3145736 | tf_op jit(solution)/shard_map/ppermute | solution.py:10
  156.9 28.3 %collective-permute-done.1 = bf16[2048,256]{1,0:T(8,128)(2,1)} collective-permute-done((bf16[2048,256]{1,0:T(8,128)(2,1)}, bf16[2048,256]{1,0:T(8,128)(2,1)}, u32[]{:S(2)}, u32[]{:S(2)}) %collective-permute-start.1) | collective-permute-done | bytes 1048608 | tf_op jit(solution)/shard_map/ppermute | solution.py:10
  185.1 7.2 %gather_fusion.4 = bf16[96,128,256]{2,1,0:T(8,128)(2,1)} fusion(bf16[16,128,256]{2,1,0:T(8,128)(2,1)} %bitcast.31, s32[1024]{0:T(1024)S(1)} %pad_clamp_fusion.1), kind=kCustom, calls=%fused_computation.3.clone | custom fusion | bytes 12583296 | tf_op jit(solution)/shard_map/jit(_take)/gather | solution.py:38
  192.3 6.0 %fusion.39 = bf16[16,256,128]{1,2,0:T(8,128)(2,1)} fusion(bf16[16,128,128]{2,1,0:T(8,128)(2,1)} %param.18, bf16[16,128,256]{2,1,0:T(8,128)(2,1)} %bitcast.140, bf16[16,6,128,128]{3,2,1,0:T(8,128)(2,1)S(1)} %copy-done, bf16[16,6,128,256]{3,2,1,0:T(8,128)(2,1)} %bitcast.130, pred[16,6]{1,0:T(8,128)(4,1)S(1)} %copy.17), kind=kOutput, calls=%fused_computation.37 | convolution fusion | flops 944766976 | bytes 12058720 | tf_op jit(solution)/shard_map/iab,ibc->iac/dot_general | solution.py:46
  198.3 3.2 %gather_fusion.5 = bf16[32,128,256]{2,1,0:T(8,128)(2,1)} fusion(bf16[16,128,256]{2,1,0:T(8,128)(2,1)} %bitcast.128, s32[1024]{0:T(1024)S(1)} %pad_clamp_fusion), kind=kCustom, calls=%fused_computation.5.clone | custom fusion | bytes 4194432 | tf_op jit(solution)/shard_map/jit(_take)/gather | solution.py:49
  201.6 0.0 copy-start.1
  201.6 3.4 %fusion.84 = bf16[4,256,128]{1,2,0:T(8,128)(2,1)} fusion(bf16[4,128,128]{2,1,0:T(8,128)(2,1)S(1)} %copy-done.2, bf16[4,8,128,128]{3,2,1,0:T(8,128)(2,1)} %param.20, bf16[4,8,128,256]{3,2,1,0:T(8,128)(2,1)} %bitcast.133, pred[4,8]{1,0:T(4,128)(4,1)S(1)} %compare_and_fusion.1, bf16[4,128,256]{2,1,0:T(8,128)(2,1)} %bitcast.143), kind=kOutput, calls=%fused_computation.52 | convolution fusion | flops 303562752 | bytes 3801120 | tf_op jit(solution)/shard_map/jab,jbc->jac/dot_general | solution.py:57
  205.0 0.0 copy-done.1
  205.0 2.0 pad_maximum_fusion.1
  206.9 3.1 %pad_maximum_fusion = bf16[2048,768]{1,0:T(8,128)(2,1)} fusion(bf16[2048,256]{1,0:T(8,128)(2,1)} %bitcast.129, bf16[2048,256]{1,0:T(8,128)(2,1)} %bitcast.127, bf16[2048,256]{1,0:T(8,128)(2,1)} %bitcast.125), kind=kLoop, calls=%fused_computation.15 | loop fusion | flops 9437184 | bytes 6291456 | tf_op jit(solution)/shard_map/concatenate | solution.py:65
  (2 shorter events, 0.0 us)
Async XLA Ops:
  7.2 36.4 %copy-start = (bf16[16,6,128,128]{3,2,1,0:T(8,128)(2,1)S(1)}, bf16[16,6,128,128]{3,2,1,0:T(8,128)(2,1)}, u32[]{:S(2)}) copy-start(bf16[16,6,128,128]{3,2,1,0:T(8,128)(2,1)} %param.17) | copy-start | bytes 9437188
  7.2 29.1 %all-gather.4.cloned.1.call-start = ((), (), s32[]{:S(2)}) async-start(), calls=%async_computation | async-start | bytes 1310720 | tf_op jit(solution)/shard_map/all_gather | solution.py:14
  7.9 72.6 %all-gather.6.cloned.1.call-start = ((), (), s32[]{:S(2)}) async-start(), calls=%async_computation.1 | async-start | bytes 1310720 | tf_op jit(solution)/shard_map/all_gather | solution.py:14
  49.6 3.3 %copy-start.2 = (bf16[4,128,128]{2,1,0:T(8,128)(2,1)S(1)}, bf16[4,128,128]{2,1,0:T(8,128)(2,1)}, u32[]{:S(2)}) copy-start(bf16[4,128,128]{2,1,0:T(8,128)(2,1)} %param.21) | copy-start | bytes 393220
  56.3 97.3 %all-gather.8.cloned.1.call-start = ((), (), s32[]{:S(2)}) async-start(), calls=%async_computation.2 | async-start | bytes 1310720 | tf_op jit(solution)/shard_map/all_gather | solution.py:14
  80.5 31.6 %collective-permute-start = (bf16[2048,256]{1,0:T(8,128)(2,1)}, bf16[2048,256]{1,0:T(8,128)(2,1)}, u32[]{:S(2)}, u32[]{:S(2)}) collective-permute-start(bf16[2048,256]{1,0:T(8,128)(2,1)} %all-gather.6.cloned.1.call-done), channel_id=1, source_target_pairs={{0,4},{4,8},{8,12},{12,16},{16,20},{20,24},{24,28},{28,32},{32,36}... | collective-permute-start | bytes 3145736 | tf_op jit(solution)/shard_map/ppermute | solution.py:10
  153.5 31.6 %collective-permute-start.1 = (bf16[2048,256]{1,0:T(8,128)(2,1)}, bf16[2048,256]{1,0:T(8,128)(2,1)}, u32[]{:S(2)}, u32[]{:S(2)}) collective-permute-start(bf16[2048,256]{1,0:T(8,128)(2,1)} %all-gather.8.cloned.1.call-done), channel_id=1, source_target_pairs={{0,4},{4,8},{8,12},{12,16},{16,20},{20,24},{24,28},{28,32},{32,36}... | collective-permute-start | bytes 3145736 | tf_op jit(solution)/shard_map/ppermute | solution.py:10
  201.6 3.4 %copy-start.1 = (bf16[4,256,128]{1,2,0:T(8,128)(2,1)S(1)}, bf16[4,256,128]{1,2,0:T(8,128)(2,1)}, u32[]{:S(2)}) copy-start(bf16[4,256,128]{1,2,0:T(8,128)(2,1)} %fusion.90) | copy-start | bytes 786436
Sparse Core Ops, SparseCore 0:
  9.8 26.4 all-gather.3
  56.4 24.0 all-gather.5
  132.2 21.2 all-gather.7
where the time goes:
time: 217 us
  waiting for transfers between devices  123 us (57%)
  local copies, waits for them, and re-layouts  37.3 us (17%)
  matrix products  28.3 us (13%)
  between operations  13.8 us (6%)
  other arithmetic  8.01 us (4%)
  starting transfers between devices  6.64 us (3%)
    all_gather x3, waiting for transfers between devices, collect(): return lax.all_gather(share, 'sub', axis=0, tiled=True)  65.1 us
    ppermute x2, waiting for transfers between devices, passed_along(): return lax.ppermute(x, axis, pairs)  56.7 us
    gather x3, local copies, waits for them, and re-layouts, shards(): picked = jnp.take(front_blocks, inner_index, axis=0)  21.6 us
    dot_general x3, matrix products, shards(): jnp.einsum('iab,ibc->iac', inner_inverse, inner_values, preferred_element...  18.1 us
    dot_general x3, matrix products, shards(): jnp.einsum('jab,jbc->jac', front_inverse, outer_values, preferred_element...  10.2 us
    gather x3, local copies, waits for them, and re-layouts, shards(): chosen = jnp.take(solved, outer_index, axis=0)  9.7 us
    ppermute x2, starting transfers between devices, passed_along(): return lax.ppermute(x, axis, pairs)  6.52 us
  transfers between devices with their start and end apart: 5, of which 5 were waited for; matrix products, arithmetic and copies ran while one was open for 4% of the time, Pallas kernels for 0%

commit v1 on v0

--- a/solution.py
+++ b/solution.py
@@ -11,7 +11,9 @@
 
 
 def collect(share):
-    return lax.all_gather(share, "sub", axis=0, tiled=True)
+    return jnp.concatenate(
+        lax.all_to_all(jnp.stack([share] * lax.axis_size("sub")), "sub", 0, 0), axis=0
+    )
 
 
 def shards(

time: 217 us -> 185 us (0.85)
  waiting for transfers between devices: 123 us -> 64.5 us
  blocking collectives: 0 us -> 34.2 us
  between operations: 13.8 us -> 0.73 us
  starting transfers between devices: 6.64 us -> 10.5 us
  local copies, waits for them, and re-layouts: 37.3 us -> 40.7 us
  other arithmetic: 8.01 us -> 5.12 us
    all_gather x3 -> x0, waiting for transfers between devices: 65.1 us -> none  [collect(): return lax.all_gather(share, 'sub', axis=0, tiled=True)]
    all_to_all x0 -> x2, blocking collectives: none -> 34.2 us  [collect(): lax.all_to_all(jnp.stack([share] * lax.axis_size('sub')), 'sub', 0, 0)]
    all_to_all x0 -> x1, waiting for transfers between devices: none -> 7.52 us  [collect(): lax.all_to_all(jnp.stack([share] * lax.axis_size('sub')), 'sub', 0, 0)]
    all_to_all x0 -> x1, starting transfers between devices: none -> 4.87 us  [collect(): lax.all_to_all(jnp.stack([share] * lax.axis_size('sub')), 'sub', 0, 0)]
    another operation x0 -> x3, local copies, waits for them, and re-layouts: none -> 3.31 us  [collect(): jnp.stack([share] * lax.axis_size('sub'))]
  transfers between devices with their start and end apart: 5 -> 3, of which waited for: 5 -> 3; matrix products, arithmetic and copies ran while one was open for 4% -> 3% of each run, Pallas kernels for 0% -> 0%
where the time goes in v1:
time: 185 us; the launch traced here: 183 us
  waiting for transfers between devices  64.5 us (35%)
  local copies, waits for them, and re-layouts  40.7 us (22%)
  blocking collectives  34.2 us (18%)
  matrix products  27.5 us (15%)
  starting transfers between devices  10.5 us (6%)
  other arithmetic  5.12 us (3%)
    ppermute x2, waiting for transfers between devices, passed_along(): return lax.ppermute(x, axis, pairs)  56.9 us
    all_to_all x2, blocking collectives, collect(): lax.all_to_all(jnp.stack([share] * lax.axis_size('sub')), 'sub', 0, 0)  34.2 us
    gather x3, local copies, waits for them, and re-layouts, shards(): picked = jnp.take(front_blocks, inner_index, axis=0)  21.7 us
    dot_general x3, matrix products, shards(): jnp.einsum('iab,ibc->iac', inner_inverse, inner_values, preferred_element...  18.1 us
    gather x3, local copies, waits for them, and re-layouts, shards(): chosen = jnp.take(solved, outer_index, axis=0)  9.7 us
    dot_general x3, matrix products, shards(): jnp.einsum('jab,jbc->jac', front_inverse, outer_values, preferred_element...  9.46 us
    all_to_all x1, waiting for transfers between devices, collect(): lax.all_to_all(jnp.stack([share] * lax.axis_size('sub')), 'sub', 0, 0)  7.52 us
    ppermute x2, starting transfers between devices, passed_along(): return lax.ppermute(x, axis, pairs)  5.64 us
  transfers between devices with their start and end apart: 3, of which 3 were waited for; matrix products, arithmetic and copies ran while one was open for 3% of the time, Pallas kernels for 0%

profile of v1, /device:TPU:9, one launch (start us, length us, event | category | flops | bytes accessed | tf_op | source)
XLA Modules:
  0.0 183.3 jit_solution(7949904036880430782)
XLA Ops:
  0.6 0.0 copy-start
  0.6 0.0 copy-start.1
  0.7 0.0 copy-start.2
  0.7 2.2 %stack.6 = bf16[4,512,256]{2,1,0:T(8,128)(2,1)} broadcast(bf16[512,256]{1,0:T(8,128)(2,1)} %param.15), dimensions={1,2} | broadcast | bytes 1310720 | tf_op jit(solution)/shard_map/stack | solution.py:15
  2.9 4.9 %all-to-all-start = ((bf16[4,512,256]{2,1,0:T(8,128)(2,1)}), bf16[4,512,256]{2,1,0:T(8,128)(2,1)}, u32[]{:S(2)}, u32[]{:S(2)}) async-start(bf16[4,512,256]{2,1,0:T(8,128)(2,1)} %stack.6), calls=%async_computation | async-start | bytes 2097152 | tf_op jit(solution)/shard_map/all_to_all | solution.py:15
  7.8 0.0 copy-done.1
  7.8 0.0 copy-done.2
  7.8 0.1 reshape.142
  7.9 0.1 copy.18
  8.0 0.1 reshape.138
  8.1 2.0 %fusion.115 = (bf16[512,256]{1,0:T(8,128)(2,1)}, bf16[512,256]{1,0:T(8,128)(2,1)}, bf16[512,256]{1,0:T(8,128)(2,1)}) fusion(bf16[512,768]{1,0:T(8,128)(2,1)} %param.14), kind=kLoop, calls=%fused_computation.75 | loop fusion | bytes 1572864 | tf_op jit(solution)/shard_map/slice | solution.py:55
  10.1 0.1 copy.17
  10.2 3.6 %fusion.114 = (bf16[2048,256]{1,0:T(8,128)(2,1)}, bf16[2048,256]{1,0:T(8,128)(2,1)}, bf16[2048,256]{1,0:T(8,128)(2,1)}) fusion(bf16[2048,768]{1,0:T(8,128)(2,1)} %param.13), kind=kLoop, calls=%fused_computation.74 | loop fusion | bytes 6291456 | tf_op jit(solution)/shard_map/slice | solution.py:44
  13.8 7.5 %all-to-all-done = bf16[4,512,256]{2,1,0:T(8,128)(2,1)} async-done(((bf16[4,512,256]{2,1,0:T(8,128)(2,1)}), bf16[4,512,256]{2,1,0:T(8,128)(2,1)}, u32[]{:S(2)}, u32[]{:S(2)}) %all-to-all-start) | async-done | bytes 1048608 | tf_op jit(solution)/shard_map/all_to_all | solution.py:15
  21.3 7.2 %gather_fusion = bf16[96,128,256]{2,1,0:T(8,128)(2,1)} fusion(bf16[16,128,256]{2,1,0:T(8,128)(2,1)} %bitcast.1, s32[1024]{0:T(1024)S(1)} %pad_clamp_fusion.1), kind=kCustom, calls=%fused_computation.clone | custom fusion | bytes 12583296 | tf_op jit(solution)/shard_map/jit(_take)/gather | solution.py:40
  28.6 0.0 copy-done
  28.6 6.0 %fusion.45 = bf16[16,256,128]{1,2,0:T(8,128)(2,1)} fusion(bf16[16,128,128]{2,1,0:T(8,128)(2,1)} %param.18, bf16[16,128,256]{2,1,0:T(8,128)(2,1)} %bitcast.145, bf16[16,6,128,128]{3,2,1,0:T(8,128)(2,1)S(1)} %copy-done, bf16[16,6,128,256]{3,2,1,0:T(8,128)(2,1)} %bitcast.132, pred[16,6]{1,0:T(8,128)(4,1)S(1)} %copy.17), kind=kOutput, calls=%fused_computation.39 | convolution fusion | flops 944766976 | bytes 12058720 | tf_op jit(solution)/shard_map/iab,ibc->iac/dot_general | solution.py:48
  34.6 0.0 copy-start.3
  34.6 3.3 %gather_fusion.1 = bf16[32,128,256]{2,1,0:T(8,128)(2,1)} fusion(bf16[16,128,256]{2,1,0:T(8,128)(2,1)} %bitcast.125, s32[1024]{0:T(1024)S(1)} %pad_clamp_fusion), kind=kCustom, calls=%fused_computation.1.clone | custom fusion | bytes 4194432 | tf_op jit(solution)/shard_map/jit(_take)/gather | solution.py:51
  37.8 0.0 copy-done.3
  37.8 2.7 %fusion.90 = bf16[4,256,128]{1,2,0:T(8,128)(2,1)S(1)} fusion(bf16[4,128,128]{2,1,0:T(8,128)(2,1)S(1)} %copy-done.3, bf16[4,8,128,128]{3,2,1,0:T(8,128)(2,1)} %param.20, bf16[4,8,128,256]{3,2,1,0:T(8,128)(2,1)} %bitcast.135, pred[4,8]{1,0:T(4,128)(4,1)S(1)} %compare_and_fusion.1, bf16[4,128,256]{2,1,0:T(8,128)(2,1)} %bitcast.148), kind=kOutput, calls=%fused_computation.54 | convolution fusion | flops 303562752 | bytes 3801120 | tf_op jit(solution)/shard_map/jab,jbc->jac/dot_general | solution.py:59
  40.5 0.1 stack.14
  40.6 16.8 %all_to_all.15 = bf16[4,512,256]{2,1,0:T(8,128)(2,1)S(1)} all-to-all(bf16[4,512,256]{2,1,0:T(8,128)(2,1)S(1)} %stack.14), channel_id=1, replica_groups=mesh['slab'=64,'sub'=4] {'sub'}, dimensions={0} | all-to-all | bytes 2097152 | tf_op jit(solution)/shard_map/all_to_all | solution.py:15
  57.4 3.5 %collective-permute-start = (bf16[2048,256]{1,0:T(8,128)(2,1)S(1)}, bf16[2048,256]{1,0:T(8,128)(2,1)}, u32[]{:S(2)}, u32[]{:S(2)}) collective-permute-start(bf16[2048,256]{1,0:T(8,128)(2,1)S(1)} %bitcast.137), channel_id=1, source_target_pairs={{0,4},{4,8},{8,12},{12,16},{16,20},{20,24},{24,28},{28,32},{32,36}... | collective-permute-start | bytes 3145736 | tf_op jit(solution)/shard_map/ppermute | solution.py:10
  61.0 28.9 %collective-permute-done = bf16[2048,256]{1,0:T(8,128)(2,1)} collective-permute-done((bf16[2048,256]{1,0:T(8,128)(2,1)S(1)}, bf16[2048,256]{1,0:T(8,128)(2,1)}, u32[]{:S(2)}, u32[]{:S(2)}) %collective-permute-start) | collective-permute-done | bytes 1048608 | tf_op jit(solution)/shard_map/ppermute | solution.py:10
  89.8 7.2 %gather_fusion.2 = bf16[96,128,256]{2,1,0:T(8,128)(2,1)} fusion(bf16[16,128,256]{2,1,0:T(8,128)(2,1)} %bitcast.17, s32[1024]{0:T(1024)S(1)} %pad_clamp_fusion.1), kind=kCustom, calls=%fused_computation.2.clone | custom fusion | bytes 12583296 | tf_op jit(solution)/shard_map/jit(_take)/gather | solution.py:40
  97.0 6.1 %fusion.42 = bf16[16,256,128]{1,2,0:T(8,128)(2,1)} fusion(bf16[16,128,128]{2,1,0:T(8,128)(2,1)} %param.18, bf16[16,128,256]{2,1,0:T(8,128)(2,1)} %bitcast.144, bf16[16,6,128,128]{3,2,1,0:T(8,128)(2,1)S(1)} %copy-done, bf16[16,6,128,256]{3,2,1,0:T(8,128)(2,1)} %bitcast.133, pred[16,6]{1,0:T(8,128)(4,1)S(1)} %copy.17), kind=kOutput, calls=%fused_computation.38 | convolution fusion | flops 944766976 | bytes 12058720 | tf_op jit(solution)/shard_map/iab,ibc->iac/dot_general | solution.py:48
  103.1 3.2 %gather_fusion.3 = bf16[32,128,256]{2,1,0:T(8,128)(2,1)} fusion(bf16[16,128,256]{2,1,0:T(8,128)(2,1)} %bitcast.127, s32[1024]{0:T(1024)S(1)} %pad_clamp_fusion), kind=kCustom, calls=%fused_computation.4.clone | custom fusion | bytes 4194432 | tf_op jit(solution)/shard_map/jit(_take)/gather | solution.py:51
  106.3 3.4 %fusion.87 = bf16[4,256,128]{1,2,0:T(8,128)(2,1)} fusion(bf16[4,128,128]{2,1,0:T(8,128)(2,1)S(1)} %copy-done.3, bf16[4,8,128,128]{3,2,1,0:T(8,128)(2,1)} %param.20, bf16[4,8,128,256]{3,2,1,0:T(8,128)(2,1)} %bitcast.136, pred[4,8]{1,0:T(4,128)(4,1)S(1)} %compare_and_fusion.1, bf16[4,128,256]{2,1,0:T(8,128)(2,1)} %bitcast.147), kind=kOutput, calls=%fused_computation.53 | convolution fusion | flops 303562752 | bytes 3801120 | tf_op jit(solution)/shard_map/jab,jbc->jac/dot_general | solution.py:59
  109.7 1.0 stack.15
  110.8 17.4 %all_to_all.16 = bf16[4,512,256]{2,1,0:T(8,128)(2,1)S(1)} all-to-all(bf16[4,512,256]{2,1,0:T(8,128)(2,1)S(1)} %stack.15), channel_id=1, replica_groups=mesh['slab'=64,'sub'=4] {'sub'}, dimensions={0} | all-to-all | bytes 2097152 | tf_op jit(solution)/shard_map/all_to_all | solution.py:15
  128.2 2.1 %collective-permute-start.1 = (bf16[2048,256]{1,0:T(8,128)(2,1)S(1)}, bf16[2048,256]{1,0:T(8,128)(2,1)}, u32[]{:S(2)}, u32[]{:S(2)}) collective-permute-start(bf16[2048,256]{1,0:T(8,128)(2,1)S(1)} %bitcast.138), channel_id=1, source_target_pairs={{0,4},{4,8},{8,12},{12,16},{16,20},{20,24},{24,28},{28,32},{32,36}... | collective-permute-start | bytes 3145736 | tf_op jit(solution)/shard_map/ppermute | solution.py:10
  130.3 28.1 %collective-permute-done.1 = bf16[2048,256]{1,0:T(8,128)(2,1)} collective-permute-done((bf16[2048,256]{1,0:T(8,128)(2,1)S(1)}, bf16[2048,256]{1,0:T(8,128)(2,1)}, u32[]{:S(2)}, u32[]{:S(2)}) %collective-permute-start.1) | collective-permute-done | bytes 1048608 | tf_op jit(solution)/shard_map/ppermute | solution.py:10
  158.4 7.2 %gather_fusion.4 = bf16[96,128,256]{2,1,0:T(8,128)(2,1)} fusion(bf16[16,128,256]{2,1,0:T(8,128)(2,1)} %bitcast.33, s32[1024]{0:T(1024)S(1)} %pad_clamp_fusion.1), kind=kCustom, calls=%fused_computation.3.clone | custom fusion | bytes 12583296 | tf_op jit(solution)/shard_map/jit(_take)/gather | solution.py:40
  165.6 6.0 %fusion.39 = bf16[16,256,128]{1,2,0:T(8,128)(2,1)} fusion(bf16[16,128,128]{2,1,0:T(8,128)(2,1)} %param.18, bf16[16,128,256]{2,1,0:T(8,128)(2,1)} %bitcast.143, bf16[16,6,128,128]{3,2,1,0:T(8,128)(2,1)S(1)} %copy-done, bf16[16,6,128,256]{3,2,1,0:T(8,128)(2,1)} %bitcast.131, pred[16,6]{1,0:T(8,128)(4,1)S(1)} %copy.17), kind=kOutput, calls=%fused_computation.37 | convolution fusion | flops 944766976 | bytes 12058720 | tf_op jit(solution)/shard_map/iab,ibc->iac/dot_general | solution.py:48
  171.6 3.2 %gather_fusion.5 = bf16[32,128,256]{2,1,0:T(8,128)(2,1)} fusion(bf16[16,128,256]{2,1,0:T(8,128)(2,1)} %bitcast.129, s32[1024]{0:T(1024)S(1)} %pad_clamp_fusion), kind=kCustom, calls=%fused_computation.5.clone | custom fusion | bytes 4194432 | tf_op jit(solution)/shard_map/jit(_take)/gather | solution.py:51
  174.8 3.4 %fusion.84 = bf16[4,256,128]{1,2,0:T(8,128)(2,1)} fusion(bf16[4,128,128]{2,1,0:T(8,128)(2,1)S(1)} %copy-done.3, bf16[4,8,128,128]{3,2,1,0:T(8,128)(2,1)} %param.20, bf16[4,8,128,256]{3,2,1,0:T(8,128)(2,1)} %bitcast.134, pred[4,8]{1,0:T(4,128)(4,1)S(1)} %compare_and_fusion.1, bf16[4,128,256]{2,1,0:T(8,128)(2,1)} %bitcast.146), kind=kOutput, calls=%fused_computation.52 | convolution fusion | flops 303562752 | bytes 3801120 | tf_op jit(solution)/shard_map/jab,jbc->jac/dot_general | solution.py:59
  178.2 2.0 %pad_maximum_fusion.1 = bf16[512,768]{1,0:T(8,128)(2,1)} fusion(bf16[512,256]{1,0:T(8,128)(2,1)} %bitcast.149, bf16[512,256]{1,0:T(8,128)(2,1)} %bitcast.142, bf16[512,256]{1,0:T(8,128)(2,1)S(1)} %bitcast.140), kind=kLoop, calls=%fused_computation.58 | loop fusion | flops 2359296 | bytes 1572864 | tf_op jit(solution)/shard_map/concatenate | solution.py:68
  180.2 3.1 %pad_maximum_fusion = bf16[2048,768]{1,0:T(8,128)(2,1)} fusion(bf16[2048,256]{1,0:T(8,128)(2,1)} %bitcast.130, bf16[2048,256]{1,0:T(8,128)(2,1)} %bitcast.128, bf16[2048,256]{1,0:T(8,128)(2,1)} %bitcast.126), kind=kLoop, calls=%fused_computation.15 | loop fusion | flops 9437184 | bytes 6291456 | tf_op jit(solution)/shard_map/concatenate | solution.py:67
  (6 shorter events, 0.0 us)
Async XLA Ops:
  0.6 27.9 %copy-start = (bf16[16,6,128,128]{3,2,1,0:T(8,128)(2,1)S(1)}, bf16[16,6,128,128]{3,2,1,0:T(8,128)(2,1)}, u32[]{:S(2)}) copy-start(bf16[16,6,128,128]{3,2,1,0:T(8,128)(2,1)} %param.17) | copy-start | bytes 9437188
  0.6 7.1 %copy-start.1 = (s32[16,6]{0,1:T(8,128)S(1)}, s32[16,6]{0,1:T(8,128)}, u32[]{:S(2)}) copy-start(s32[16,6]{0,1:T(8,128)} %param.16) | copy-start | bytes 1156
  0.7 7.1 %copy-start.2 = (s32[4,8]{1,0:T(4,128)S(1)}, s32[4,8]{1,0:T(4,128)}, u32[]{:S(2)}) copy-start(s32[4,8]{1,0:T(4,128)} %param.19) | copy-start | bytes 388
  2.9 18.4 %all-to-all-start = ((bf16[4,512,256]{2,1,0:T(8,128)(2,1)}), bf16[4,512,256]{2,1,0:T(8,128)(2,1)}, u32[]{:S(2)}, u32[]{:S(2)}) async-start(bf16[4,512,256]{2,1,0:T(8,128)(2,1)} %stack.6), calls=%async_computation | async-start | bytes 2097152 | tf_op jit(solution)/shard_map/all_to_all | solution.py:15
  34.6 3.3 %copy-start.3 = (bf16[4,128,128]{2,1,0:T(8,128)(2,1)S(1)}, bf16[4,128,128]{2,1,0:T(8,128)(2,1)}, u32[]{:S(2)}) copy-start(bf16[4,128,128]{2,1,0:T(8,128)(2,1)} %param.21) | copy-start | bytes 393220
  57.4 32.4 %collective-permute-start = (bf16[2048,256]{1,0:T(8,128)(2,1)S(1)}, bf16[2048,256]{1,0:T(8,128)(2,1)}, u32[]{:S(2)}, u32[]{:S(2)}) collective-permute-start(bf16[2048,256]{1,0:T(8,128)(2,1)S(1)} %bitcast.137), channel_id=1, source_target_pairs={{0,4},{4,8},{8,12},{12,16},{16,20},{20,24},{24,28},{28,32},{32,36}... | collective-permute-start | bytes 3145736 | tf_op jit(solution)/shard_map/ppermute | solution.py:10
  128.2 30.2 %collective-permute-start.1 = (bf16[2048,256]{1,0:T(8,128)(2,1)S(1)}, bf16[2048,256]{1,0:T(8,128)(2,1)}, u32[]{:S(2)}, u32[]{:S(2)}) collective-permute-start(bf16[2048,256]{1,0:T(8,128)(2,1)S(1)} %bitcast.138), channel_id=1, source_target_pairs={{0,4},{4,8},{8,12},{12,16},{16,20},{20,24},{24,28},{28,32},{32,36}... | collective-permute-start | bytes 3145736 | tf_op jit(solution)/shard_map/ppermute | solution.py:10
